TPU v7x, 512 devices: a whole 4x8x8 slice. The times are simulated.
512 devices in a mesh: gx: 8 (over y_lo, x), gy: 4 (over y_hi), gz: 16 (over z, core).
Axes of the slice: x: 4, y: 8 (y_hi: 4, y_lo: 2; y = y_hi * 2 + y_lo), z: 8, core: 2. Of those that a mesh axis runs over, the one named last changes fastest.
Arguments:
- source_term: float32 [64, 64, 2048], P('gx', 'gy', 'gz'), may hold values from -6 to 6
- conductivity: float32 [64, 64, 2048], P('gx', 'gy', 'gz'), may hold values from 0.3 to 3
- initial_guess: float32 [64, 64, 2048], P('gx', 'gy', 'gz'), may hold values from -4 to 4
- box_owner: int32 [8, 4, 16], replicated, may hold values from 0 to 3
Outputs:
- potential: float32 [64, 64, 2048], P('gx', 'gy', 'gz')
Inputs may be any that keep to these rules, and one draw needn't show every extreme that they name: `box_owner`: labels of the coarse boxes; boxes with equal labels couple only within one plane of boxes along z.
All inputs are finite; a program needn't handle non-finite values.
Results may differ from a plain program's by a relative error of at most 0.0001.
Values sent between devices are 32-bit elements; how exact they have to be, the bound alone decides.
A program may use at most 64 MiB of HBM per device.

v0:
```python
import jax
import jax.numpy as jnp
from jax import lax
from jax.sharding import PartitionSpec as P

CSWEEPS = 8
screening = 0.05


def with_halo(block, sides, width):
    for axis, dim in sides:
        count = lax.axis_size(axis)
        forward = [(i, i + 1) for i in range(count - 1)]
        forward.append((count - 1, 0))
        backward = [(target, source) for source, target in forward]
        low = lax.ppermute(
            lax.slice_in_dim(block, block.shape[dim] - width, None, axis=dim), axis, forward
        )
        high = lax.ppermute(lax.slice_in_dim(block, 0, width, axis=dim), axis, backward)
        block = jnp.concatenate([low, block, high], axis=dim)
    return block


def coarsen(values):
    extent = values.shape
    return values.reshape(extent[0] // 2, 2, extent[1] // 2, 2, extent[2] // 2, 2).mean(
        axis=(1, 3, 5)
    )


def refine(values):
    return jnp.repeat(jnp.repeat(jnp.repeat(values, 2, 0), 2, 1), 2, 2)


def trimmed(values, margin):
    return values[margin:-margin, margin:-margin, margin:-margin]


def weights_from(padded, stiffness):
    centre = padded[1:-1, 1:-1, 1:-1]
    weights = (
        (centre + padded[2:, 1:-1, 1:-1]) * 0.5,
        (centre + padded[:-2, 1:-1, 1:-1]) * 0.5,
        (centre + padded[1:-1, 2:, 1:-1]) * 0.5,
        (centre + padded[1:-1, :-2, 1:-1]) * 0.5,
        (centre + padded[1:-1, 1:-1, 2:]) * 0.5,
        (centre + padded[1:-1, 1:-1, :-2]) * 0.5,
    )
    diagonal = screening + stiffness * (
        weights[0] + weights[1] + weights[2] + weights[3] + weights[4] + weights[5]
    )
    return (weights, diagonal)


def neighbour_sum(padded, weights, margin):
    parts = [trimmed(values, margin) for values in weights]
    return (
        parts[0] * padded[2:, 1:-1, 1:-1]
        + parts[1] * padded[:-2, 1:-1, 1:-1]
        + parts[2] * padded[1:-1, 2:, 1:-1]
        + parts[3] * padded[1:-1, :-2, 1:-1]
        + parts[4] * padded[1:-1, 1:-1, 2:]
        + parts[5] * padded[1:-1, 1:-1, :-2]
    )


def relax_cells(padded, depth, level_data, colour):
    weights, diagonal, source_ext, parity_ext, stiffness = level_data
    margin = 2 - depth
    centre = padded[1:-1, 1:-1, 1:-1]
    nearby = neighbour_sum(padded, weights, margin)
    updated = (trimmed(source_ext, margin) + stiffness * nearby) / trimmed(diagonal, margin)
    return jnp.where(trimmed(parity_ext, margin) == colour, updated, centre)


def smooth(field, level_data):
    for colour in (0, 1):
        padded = with_halo(field, (("gx", 0), ("gy", 1), ("gz", 2)), 1)
        field = relax_cells(padded, 1, level_data, colour)
    return field


def level_setup(coef, source, stiffness):
    coef_ext = jnp.pad(with_halo(coef, (("gx", 0), ("gy", 1), ("gz", 2)), 1), 1)
    source_ext = jnp.pad(source, 1)
    weights, diagonal = weights_from(coef_ext, stiffness)
    extent = source.shape
    x_index = jnp.arange(extent[0] + 2, dtype=jnp.int32) + lax.axis_index("gx") * extent[0] - 1
    y_index = jnp.arange(extent[1] + 2, dtype=jnp.int32) + lax.axis_index("gy") * extent[1] - 1
    z_index = jnp.arange(extent[2] + 2, dtype=jnp.int32) + lax.axis_index("gz") * extent[2] - 1
    parity_ext = (x_index[:, None, None] + y_index[None, :, None] + z_index[None, None, :]) % 2
    return (weights, diagonal, source_ext, parity_ext, stiffness)


def beside_all(field, weights):
    return (
        weights[0] * jnp.roll(field, -1, 0)
        + weights[1] * jnp.roll(field, 1, 0)
        + weights[2] * jnp.roll(field, -1, 1)
        + weights[3] * jnp.roll(field, 1, 1)
        + weights[4] * jnp.roll(field, -1, 2)
        + weights[5] * jnp.roll(field, 1, 2)
    )


def coarse_solve(source, diagonal, weights, labels, box_depth, stiffness):
    extent = source.shape
    z_local = jnp.arange(extent[2], dtype=jnp.int32) % box_depth
    z_up = jnp.broadcast_to((z_local != box_depth - 1)[None, None, :], extent)
    z_down = jnp.broadcast_to((z_local != 0)[None, None, :], extent)
    masks = (
        labels == jnp.roll(labels, -1, 0),
        labels == jnp.roll(labels, 1, 0),
        labels == jnp.roll(labels, -1, 1),
        labels == jnp.roll(labels, 1, 1),
        z_up,
        z_down,
    )
    cut_weights = tuple((weights[index] * masks[index].astype(jnp.float32) for index in range(6)))
    x_index = jnp.arange(extent[0], dtype=jnp.int32)
    y_index = jnp.arange(extent[1], dtype=jnp.int32)
    z_index = jnp.arange(extent[2], dtype=jnp.int32)
    parity = (x_index[:, None, None] + y_index[None, :, None] + z_index[None, None, :]) % 2
    correction = jnp.zeros(extent, jnp.float32)
    for _ in range(CSWEEPS):
        for colour in (0, 1):
            updated = (source + stiffness * beside_all(correction, cut_weights)) / diagonal
            correction = jnp.where(parity == colour, updated, correction)
    return correction


def assemble(gathered, boxes_x, boxes_y, boxes_z, box_extent):
    width_x, width_y, width_z = box_extent
    blocks = gathered.reshape(boxes_x, boxes_y, boxes_z, 8, width_x, width_y, width_z)
    blocks = blocks.transpose(3, 0, 4, 1, 5, 2, 6)
    return blocks.reshape(8, boxes_x * width_x, boxes_y * width_y, boxes_z * width_z)


def local(source_term, conductivity, initial_guess, box_owner):
    field = initial_guess
    source = source_term
    coef = conductivity
    saved = []
    for coarse_step in range(3):
        stiffness = 0.25**coarse_step
        level_data = level_setup(coef, source, stiffness)
        if coarse_step > 0:
            field = jnp.zeros(source.shape, jnp.float32)
        field = smooth(field, level_data)
        padded = with_halo(field, (("gx", 0), ("gy", 1), ("gz", 2)), 1)
        nearby = neighbour_sum(padded, level_data[0], 1)
        residual = source - (trimmed(level_data[1], 1) * field - stiffness * nearby)
        saved.append((field, level_data))
        source = coarsen(residual)
        coef = coarsen(coef)
    stiffness = 0.25**3
    coef_ext = with_halo(coef, (("gx", 0), ("gy", 1), ("gz", 2)), 1)
    weights, diagonal = weights_from(coef_ext, stiffness)
    box_extent = source.shape
    payload = jnp.stack((source, diagonal) + weights).reshape(
        1, 8, box_extent[0] * box_extent[1] * box_extent[2]
    )
    boxes_x = lax.axis_size("gx")
    boxes_y = lax.axis_size("gy")
    plane_index = lax.axis_index("gz")
    gathered = lax.all_gather(payload, ("gx", "gy", "gz"), axis=0, tiled=True)
    fields = assemble(gathered, boxes_x, boxes_y, lax.axis_size("gz"), box_extent)
    z_start = plane_index * box_extent[2]
    labels = jnp.repeat(
        jnp.repeat(jnp.repeat(box_owner, box_extent[0], 0), box_extent[1], 1), box_extent[2], 2
    )
    correction_all = coarse_solve(
        fields[0],
        fields[1],
        tuple((fields[index] for index in range(2, 8))),
        labels,
        box_extent[2],
        stiffness,
    )
    starts = (lax.axis_index("gx") * box_extent[0], lax.axis_index("gy") * box_extent[1], z_start)
    correction = lax.dynamic_slice(correction_all, starts, box_extent)
    for coarse_step in (2, 1, 0):
        field, level_data = saved[coarse_step]
        field = smooth(field + refine(correction), level_data)
        correction = field
    return correction


def solution(mesh):
    return jax.shard_map(
        local,
        mesh=mesh,
        in_specs=(P("gx", "gy", "gz"), P("gx", "gy", "gz"), P("gx", "gy", "gz"), P()),
        out_specs=P("gx", "gy", "gz"),
        check_vma=False,
    )
```

profile of v0, /device:TPU:8, one launch (start us, length us, event | category | flops | bytes accessed | tf_op | source)
XLA Modules:
  0.0 1306.6 jit_solution(13660067413614063454)
XLA Ops:
  0.0 4.7 collective-permute-start.30
  6.6 6.3 reshape.307
  19.2 5.2 collective-permute-start.72
  49.8 6.0 collective-permute-start.6
  57.8 6.0 collective-permute-start.25
  65.8 6.0 collective-permute-start.1
  100.2 5.1 collective-permute-start.56
  112.2 5.3 collective-permute-start.8
  119.5 5.5 collective-permute-done.9
  171.7 5.6 collective-permute-done.19
  179.6 4.4 collective-permute-start.21
  187.4 4.5 collective-permute-done.35
  196.4 4.8 collective-permute-start.51
  201.5 5.6 reshape.306
  219.9 4.3 collective-permute-start.39
  252.4 6.0 collective-permute-start.45
  311.0 4.8 collective-permute-start.69
  323.5 798.0 %all_gather.3 = f32[512,8,32]{2,1,0:T(8,128)S(1)} all-gather(f32[1,8,32]{2,1,0:T(8,128)S(1)} %stack.32), channel_id=1, replica_groups=mesh['gx'=8,'gy'=4,'gz'=16] {'gx','gy','gz'}, dimensions={0}, use_global_device_ids=true | all-gather | bytes 525312 | tf_op jit(solution)/shard_map/all_gather | solution.py:166
  1126.5 4.7 fusion.419
  1164.6 4.8 collective-permute-start.81
  1188.3 4.8 collective-permute-start.87
  1213.9 4.3 collective-permute-start.92
  1236.7 5.8 collective-permute-start.99
  1292.5 4.8 collective-permute-start.111
  (676 shorter events, 385.9 us)
Async XLA Ops:
  0.0 57.8 %collective-permute-start.30 = (f32[1,8,64]{2,1,0:T(8,128)S(1)}, f32[1,8,64]{2,1,0:T(8,128)S(1)}, u32[]{:S(2)}, u32[]{:S(2)}) collective-permute-start(f32[1,8,64]{2,1,0:T(8,128)S(1)} %broadcast.418), channel_id=1, source_target_pairs={{64,0},{128,64},{192,128},{256,192},{320,256},{384,320},{448,384},... | collective-permute-start | bytes 6152 | tf_op jit(solution)/shard_map/ppermute | solution.py:19
  4.7 59.1 %collective-permute-start.31 = (f32[1,8,64]{2,1,0:T(8,128)S(1)}, f32[1,8,64]{2,1,0:T(8,128)S(1)}, u32[]{:S(2)}, u32[]{:S(2)}) collective-permute-start(f32[1,8,64]{2,1,0:T(8,128)S(1)} %broadcast.418), channel_id=1, source_target_pairs={{0,64},{64,128},{128,192},{192,256},{256,320},{320,384},{384,448},... | collective-permute-start | bytes 6152 | tf_op jit(solution)/shard_map/ppermute | solution.py:16
  16.4 20.8 %collective-permute-start.73 = (f32[1,2,16]{2,1,0:T(2,128)S(1)}, f32[1,2,16]{2,1,0:T(2,128)S(1)}, u32[]{:S(2)}, u32[]{:S(2)}) collective-permute-start(f32[1,2,16]{2,1,0:T(2,128)S(1)} %multiply_bitcast_fusion), channel_id=1, source_target_pairs={{0,64},{64,128},{128,192},{192,256},{256,320},{320,384},{384,448},... | collective-permute-start | bytes 392 | tf_op jit(solution)/shard_map/ppermute | solution.py:16
  19.2 21.0 %collective-permute-start.72 = (f32[1,2,16]{2,1,0:T(2,128)S(1)}, f32[1,2,16]{2,1,0:T(2,128)S(1)}, u32[]{:S(2)}, u32[]{:S(2)}) collective-permute-start(f32[1,2,16]{2,1,0:T(2,128)S(1)} %multiply_bitcast_fusion), channel_id=1, source_target_pairs={{64,0},{128,64},{192,128},{256,192},{320,256},{384,320},{448,384},... | collective-permute-start | bytes 392 | tf_op jit(solution)/shard_map/ppermute | solution.py:19
  24.4 25.4 %collective-permute-start.54 = (f32[1,4,32]{2,1,0:T(4,128)S(1)}, f32[1,4,32]{2,1,0:T(4,128)S(1)}, u32[]{:S(2)}, u32[]{:S(2)}) collective-permute-start(f32[1,4,32]{2,1,0:T(4,128)S(1)} %broadcast.427), channel_id=1, source_target_pairs={{64,0},{128,64},{192,128},{256,192},{320,256},{384,320},{448,384},... | collective-permute-start | bytes 1544 | tf_op jit(solution)/shard_map/ppermute | solution.py:19
  43.1 12.7 collective-permute-start.55
  47.8 57.5 %collective-permute-start.7 = (f32[1,16,128]{2,1,0:T(8,128)S(1)}, f32[1,16,128]{2,1,0:T(8,128)S(1)}, u32[]{:S(2)}, u32[]{:S(2)}) collective-permute-start(f32[1,16,128]{2,1,0:T(8,128)S(1)} %get-tuple-element.272), channel_id=1, source_target_pairs={{0,64},{64,128},{128,192},{192,256},{256,320},{320,384},{384,448},... | collective-permute-start | bytes 24584 | tf_op jit(solution)/shard_map/ppermute | solution.py:16
  49.8 59.6 %collective-permute-start.6 = (f32[1,16,128]{2,1,0:T(8,128)S(1)}, f32[1,16,128]{2,1,0:T(8,128)S(1)}, u32[]{:S(2)}, u32[]{:S(2)}) collective-permute-start(f32[1,16,128]{2,1,0:T(8,128)S(1)} %get-tuple-element.271), channel_id=1, source_target_pairs={{64,0},{128,64},{192,128},{256,192},{320,256},{384,320},{448,384},... | collective-permute-start | bytes 24584 | tf_op jit(solution)/shard_map/ppermute | solution.py:19
  55.8 41.5 %collective-permute-start = (f32[1,16,128]{2,1,0:T(8,128)S(1)}, f32[1,16,128]{2,1,0:T(8,128)S(1)}, u32[]{:S(2)}, u32[]{:S(2)}) collective-permute-start(f32[1,16,128]{2,1,0:T(8,128)S(1)} %get-tuple-element.270), channel_id=1, source_target_pairs={{0,64},{64,128},{128,192},{192,256},{256,320},{320,384},{384,448},... | collective-permute-start | bytes 24584 | tf_op jit(solution)/shard_map/ppermute | solution.py:16
  57.8 8.0 collective-permute-start.25
  63.8 8.0 collective-permute-start.24
  65.8 34.4 %collective-permute-start.1 = (f32[1,16,128]{2,1,0:T(8,128)S(1)}, f32[1,16,128]{2,1,0:T(8,128)S(1)}, u32[]{:S(2)}, u32[]{:S(2)}) collective-permute-start(f32[1,16,128]{2,1,0:T(8,128)S(1)} %get-tuple-element.269), channel_id=1, source_target_pairs={{64,0},{128,64},{192,128},{256,192},{320,256},{384,320},{448,384},... | collective-permute-start | bytes 24584 | tf_op jit(solution)/shard_map/ppermute | solution.py:19
  93.4 185.7 %collective-permute-start.74 = (f32[3,1,16]{2,1,0:T(1,128)S(1)}, f32[3,1,16]{2,1,0:T(1,128)S(1)}, u32[]{:S(2)}, u32[]{:S(2)}) collective-permute-start(f32[3,1,16]{2,1,0:T(1,128)S(1)} %get-tuple-element.374), channel_id=1, source_target_pairs={{16,0},{32,16},{48,32},{0,48},{17,1},{33,17},{49,33},{1,49},{18,2}... | collective-permute-start | bytes 584 | tf_op jit(solution)/shard_map/ppermute | solution.py:19
  97.3 181.9 %collective-permute-start.75 = (f32[3,1,16]{2,1,0:T(1,128)S(1)}, f32[3,1,16]{2,1,0:T(1,128)S(1)}, u32[]{:S(2)}, u32[]{:S(2)}) collective-permute-start(f32[3,1,16]{2,1,0:T(1,128)S(1)} %get-tuple-element.373), channel_id=1, source_target_pairs={{0,16},{16,32},{32,48},{48,0},{1,17},{17,33},{33,49},{49,1},{2,18}... | collective-permute-start | bytes 584 | tf_op jit(solution)/shard_map/ppermute | solution.py:16
  100.2 110.2 %collective-permute-start.56 = (f32[4,1,32]{2,1,0:T(1,128)S(1)}, f32[4,1,32]{2,1,0:T(1,128)S(1)}, u32[]{:S(2)}, u32[]{:S(2)}) collective-permute-start(f32[4,1,32]{2,1,0:T(1,128)S(1)} %get-tuple-element.358), channel_id=1, source_target_pairs={{16,0},{32,16},{48,32},{0,48},{17,1},{33,17},{49,33},{1,49},{18,2}... | collective-permute-start | bytes 1544 | tf_op jit(solution)/shard_map/ppermute | solution.py:19
  125.2 10.3 collective-permute-start.11
  193.2 19.1 %collective-permute-start.57 = (f32[4,1,32]{2,1,0:T(1,128)S(1)}, f32[4,1,32]{2,1,0:T(1,128)S(1)}, u32[]{:S(2)}, u32[]{:S(2)}) collective-permute-start(f32[4,1,32]{2,1,0:T(1,128)S(1)} %get-tuple-element.357), channel_id=1, source_target_pairs={{0,16},{16,32},{32,48},{48,0},{1,17},{17,33},{33,49},{49,1},{2,18}... | collective-permute-start | bytes 1544 | tf_op jit(solution)/shard_map/ppermute | solution.py:16
  196.4 37.6 %collective-permute-start.51 = (f32[4,1,32]{2,1,0:T(1,128)S(1)}, f32[4,1,32]{2,1,0:T(1,128)S(1)}, u32[]{:S(2)}, u32[]{:S(2)}) collective-permute-start(f32[4,1,32]{2,1,0:T(1,128)S(1)} %get-tuple-element.356), channel_id=1, source_target_pairs={{16,0},{32,16},{48,32},{0,48},{17,1},{33,17},{49,33},{1,49},{18,2}... | collective-permute-start | bytes 1544 | tf_op jit(solution)/shard_map/ppermute | solution.py:19
  216.3 20.7 %collective-permute-start.50 = (f32[4,1,32]{2,1,0:T(1,128)S(1)}, f32[4,1,32]{2,1,0:T(1,128)S(1)}, u32[]{:S(2)}, u32[]{:S(2)}) collective-permute-start(f32[4,1,32]{2,1,0:T(1,128)S(1)} %get-tuple-element.355), channel_id=1, source_target_pairs={{0,16},{16,32},{32,48},{48,0},{1,17},{17,33},{33,49},{49,1},{2,18}... | collective-permute-start | bytes 1544 | tf_op jit(solution)/shard_map/ppermute | solution.py:16
  233.9 38.2 %collective-permute-start.59 = (f32[4,6,1]{2,1,0:T(8,128)S(1)}, f32[4,6,1]{2,1,0:T(8,128)S(1)}, u32[]{:S(2)}, u32[]{:S(2)}) collective-permute-start(f32[4,6,1]{2,1,0:T(8,128)S(1)} %get-tuple-element.342), channel_id=1, source_target_pairs={{0,1},{1,2},{2,3},{3,4},{4,5},{5,6},{6,7},{7,8},{8,9},{9,10},{10,1... | collective-permute-start | bytes 296 | tf_op jit(solution)/shard_map/ppermute | solution.py:16
  252.4 10.4 collective-permute-start.45
  282.8 8.2 collective-permute-start.62
  289.8 15.5 %collective-permute-start.76 = (f32[3,4,1]{2,1,0:T(4,128)S(1)}, f32[3,4,1]{2,1,0:T(4,128)S(1)}, u32[]{:S(2)}, u32[]{:S(2)}) collective-permute-start(f32[3,4,1]{2,1,0:T(4,128)S(1)} %get-tuple-element.360), channel_id=1, source_target_pairs={{1,0},{2,1},{3,2},{4,3},{5,4},{6,5},{7,6},{8,7},{9,8},{10,9},{11,1... | collective-permute-start | bytes 152 | tf_op jit(solution)/shard_map/ppermute | solution.py:19
  291.1 14.3 %collective-permute-start.77 = (f32[3,4,1]{2,1,0:T(4,128)S(1)}, f32[3,4,1]{2,1,0:T(4,128)S(1)}, u32[]{:S(2)}, u32[]{:S(2)}) collective-permute-start(f32[3,4,1]{2,1,0:T(4,128)S(1)} %get-tuple-element.359), channel_id=1, source_target_pairs={{0,1},{1,2},{2,3},{3,4},{4,5},{5,6},{6,7},{7,8},{8,9},{9,10},{10,1... | collective-permute-start | bytes 152 | tf_op jit(solution)/shard_map/ppermute | solution.py:16
  (153 other events, 4369.6 us)
where the time goes:
time: 1310 us
  blocking collectives  798 us (61%)
  starting transfers between devices  295 us (23%)
  waiting for transfers between devices  141 us (11%)
  local copies, waits for them, and re-layouts  49 us (4%)
  other arithmetic  20.4 us (2%)
    all_gather x1, blocking collectives, local(): gathered = lax.all_gather(payload, ('gx', 'gy', 'gz'), axis=0, tiled=True)  798 us
    ppermute x57, starting transfers between devices, with_halo(): lax.ppermute(lax.slice_in_dim(block, 0, width, axis=dim), axis, backward)  158 us
    ppermute x57, starting transfers between devices, with_halo(): lax.ppermute(lax.slice_in_dim(block, block.shape[dim] - width, None, axis...  137 us
    ppermute x57, waiting for transfers between devices, with_halo(): lax.ppermute(lax.slice_in_dim(block, block.shape[dim] - width, None, axis...  116 us
  transfers between devices with their start and end apart: 114, of which 51 were waited for; matrix products, arithmetic and copies ran while one was open for 3% of the time, Pallas kernels for 0%

commit v1 on v0

--- a/solution.py
+++ b/solution.py
@@ -163,7 +163,13 @@
     boxes_x = lax.axis_size("gx")
     boxes_y = lax.axis_size("gy")
     plane_index = lax.axis_index("gz")
-    gathered = lax.all_gather(payload, ("gx", "gy", "gz"), axis=0, tiled=True)
+    heap = []
+    for _ in range(lax.axis_size(("gx", "gy", "gz"))):
+        heap.append(payload)
+    gathered = jnp.concatenate(
+        lax.all_to_all(jnp.stack(heap), axis_name=("gx", "gy", "gz"), split_axis=0, concat_axis=0),
+        0,
+    )
     fields = assemble(gathered, boxes_x, boxes_y, lax.axis_size("gz"), box_extent)
     z_start = plane_index * box_extent[2]
     labels = jnp.repeat(

time: 1310 us -> 547 us (0.42)
  blocking collectives: 798 us -> 0 us
  waiting for transfers between devices: 141 us -> 159 us
    all_gather x1 -> x0, blocking collectives: 798 us -> none  [local(): gathered = lax.all_gather(payload, ('gx', 'gy', 'gz'), axis=0, tiled=True)]
    all_to_all x0 -> x1, waiting for transfers between devices: none -> 17.1 us  [local(): lax.all_to_all(jnp.stack(heap), axis_name=('gx', 'gy', 'gz'), split_axis=...]
  transfers between devices with their start and end apart: 114 -> 115, of which waited for: 51 -> 52; matrix products, arithmetic and copies ran while one was open for 3% -> 6% of each run, Pallas kernels for 0% -> 0%
where the time goes in v1:
time: 547 us; the launch traced here: 544 us
  starting transfers between devices  308 us (56%)
  waiting for transfers between devices  159 us (29%)
  local copies, waits for them, and re-layouts  51.8 us (9%)
  other arithmetic  22.3 us (4%)
    ppermute x57, starting transfers between devices, with_halo(): lax.ppermute(lax.slice_in_dim(block, 0, width, axis=dim), axis, backward)  161 us
    ppermute x57, starting transfers between devices, with_halo(): lax.ppermute(lax.slice_in_dim(block, block.shape[dim] - width, None, axis...  134 us
    ppermute x57, waiting for transfers between devices, with_halo(): lax.ppermute(lax.slice_in_dim(block, block.shape[dim] - width, None, axis...  118 us
    ppermute x57, waiting for transfers between devices, with_halo(): lax.ppermute(lax.slice_in_dim(block, 0, width, axis=dim), axis, backward)  23.5 us
    all_to_all x1, waiting for transfers between devices, local(): lax.all_to_all(jnp.stack(heap), axis_name=('gx', 'gy', 'gz'), split_axis=...  17.1 us
    reshape x3, local copies, waits for them, and re-layouts, coarsen(): values.reshape(extent[0] // 2, 2, extent[1] // 2, 2, extent[2] // 2, 2)  12.5 us
    all_to_all x1, starting transfers between devices, local(): lax.all_to_all(jnp.stack(heap), axis_name=('gx', 'gy', 'gz'), split_axis=...  12.4 us
  transfers between devices with their start and end apart: 115, of which 52 were waited for; matrix products, arithmetic and copies ran while one was open for 6% of the time, Pallas kernels for 0%

profile of v1, /device:TPU:8, one launch (start us, length us, event | category | flops | bytes accessed | tf_op | source)
XLA Modules:
  0.0 544.3 jit_solution(15667286242418150591)
XLA Ops:
  0.0 4.7 collective-permute-start.30
  6.6 6.3 %reshape.306 = f32[4,2,8,2,64,2]{5,4,3,2,1,0:T(8,128)} reshape(f32[8,16,128]{2,1,0:T(8,128)} %param.5) | data formatting | bytes 131072 | tf_op jit(solution)/shard_map/reshape | solution.py:26
  19.2 5.2 collective-permute-start.72
  44.5 6.0 %collective-permute-start.6 = (f32[1,16,128]{2,1,0:T(8,128)S(1)}, f32[1,16,128]{2,1,0:T(8,128)S(1)}, u32[]{:S(2)}, u32[]{:S(2)}) collective-permute-start(f32[1,16,128]{2,1,0:T(8,128)S(1)} %get-tuple-element.271), channel_id=1, source_target_pairs={{64,0},{128,64},{192,128},{256,192},{320,256},{384,320},{448,384},... | collective-permute-start | bytes 24584 | tf_op jit(solution)/shard_map/ppermute | solution.py:19
  52.5 6.0 %collective-permute-start.25 = (f32[1,8,64]{2,1,0:T(8,128)S(1)}, f32[1,8,64]{2,1,0:T(8,128)S(1)}, u32[]{:S(2)}, u32[]{:S(2)}) collective-permute-start(f32[1,8,64]{2,1,0:T(8,128)S(1)} %get-tuple-element.346), channel_id=1, source_target_pairs={{64,0},{128,64},{192,128},{256,192},{320,256},{384,320},{448,384},... | collective-permute-start | bytes 6152 | tf_op jit(solution)/shard_map/ppermute | solution.py:19
  60.5 6.0 %collective-permute-start.1 = (f32[1,16,128]{2,1,0:T(8,128)S(1)}, f32[1,16,128]{2,1,0:T(8,128)S(1)}, u32[]{:S(2)}, u32[]{:S(2)}) collective-permute-start(f32[1,16,128]{2,1,0:T(8,128)S(1)} %get-tuple-element.269), channel_id=1, source_target_pairs={{64,0},{128,64},{192,128},{256,192},{320,256},{384,320},{448,384},... | collective-permute-start | bytes 24584 | tf_op jit(solution)/shard_map/ppermute | solution.py:19
  95.0 5.1 collective-permute-start.56
  106.9 5.3 collective-permute-start.8
  114.3 5.5 %collective-permute-done.9 = f32[10,1,128]{2,1,0:T(1,128)S(1)} collective-permute-done((f32[10,1,128]{2,1,0:T(1,128)S(1)}, f32[10,1,128]{2,1,0:T(1,128)S(1)}, u32[]{:S(2)}, u32[]{:S(2)}) %collective-permute-start.9) | collective-permute-done | bytes 5152 | tf_op jit(solution)/shard_map/ppermute | solution.py:16
  166.4 5.6 %collective-permute-done.19 = f32[1,16,128]{2,1,0:T(8,128)S(1)} collective-permute-done((f32[1,16,128]{2,1,0:T(8,128)S(1)}, f32[1,16,128]{2,1,0:T(8,128)S(1)}, u32[]{:S(2)}, u32[]{:S(2)}) %collective-permute-start.19) | collective-permute-done | bytes 8224 | tf_op jit(solution)/shard_map/ppermute | solution.py:16
  174.4 4.4 collective-permute-start.21
  182.2 4.5 collective-permute-done.35
  191.1 4.8 collective-permute-start.51
  196.2 5.6 %reshape.305 = f32[4,2,8,2,64,2]{5,4,3,2,1,0:T(8,128)} reshape(f32[8,16,128]{2,1,0:T(8,128)S(1)} %fusion.44) | data formatting | bytes 131072 | tf_op jit(solution)/shard_map/reshape | solution.py:26
  247.2 6.0 %collective-permute-start.45 = (f32[6,1,64]{2,1,0:T(1,128)S(1)}, f32[6,1,64]{2,1,0:T(1,128)S(1)}, u32[]{:S(2)}, u32[]{:S(2)}) collective-permute-start(f32[6,1,64]{2,1,0:T(1,128)S(1)} %get-tuple-element.307), channel_id=1, source_target_pairs={{0,16},{16,32},{32,48},{48,0},{1,17},{17,33},{33,49},{49,1},{2,18}... | collective-permute-start | bytes 4616 | tf_op jit(solution)/shard_map/ppermute | solution.py:16
  305.7 5.0 collective-permute-start.69
  320.1 12.4 %all-to-all-start = ((f32[512,1,256]{2,1,0:T(1,128)}), f32[512,1,256]{2,1,0:T(1,128)S(1)}, u32[]{:S(2)}, u32[]{:S(2)}) async-start(f32[512,1,256]{2,1,0:T(1,128)} %reshape.316), calls=%async_computation | async-start | bytes 1048576 | tf_op jit(solution)/shard_map/all_to_all | solution.py:170
  337.7 17.1 %all-to-all-done = f32[512,1,256]{2,1,0:T(1,128)S(1)} async-done(((f32[512,1,256]{2,1,0:T(1,128)}), f32[512,1,256]{2,1,0:T(1,128)S(1)}, u32[]{:S(2)}, u32[]{:S(2)}) %all-to-all-start) | async-done | bytes 524320 | tf_op jit(solution)/shard_map/all_to_all | solution.py:170
  362.7 4.7 fusion.419
  395.2 5.1 collective-permute-done.79
  402.4 4.6 collective-permute-start.81
  451.8 5.1 collective-permute-start.92
  474.4 5.8 %collective-permute-start.99 = (f32[6,1,64]{2,1,0:T(1,128)S(1)}, f32[6,1,64]{2,1,0:T(1,128)S(1)}, u32[]{:S(2)}, u32[]{:S(2)}) collective-permute-start(f32[6,1,64]{2,1,0:T(1,128)S(1)} %get-tuple-element.303), channel_id=1, source_target_pairs={{0,16},{16,32},{32,48},{48,0},{1,17},{17,33},{33,49},{49,1},{2,18}... | collective-permute-start | bytes 4616 | tf_op jit(solution)/shard_map/ppermute | solution.py:16
  530.2 4.8 collective-permute-start.111
  (682 shorter events, 395.3 us)
Async XLA Ops:
  0.0 52.5 %collective-permute-start.30 = (f32[1,8,64]{2,1,0:T(8,128)S(1)}, f32[1,8,64]{2,1,0:T(8,128)S(1)}, u32[]{:S(2)}, u32[]{:S(2)}) collective-permute-start(f32[1,8,64]{2,1,0:T(8,128)S(1)} %broadcast.420), channel_id=1, source_target_pairs={{64,0},{128,64},{192,128},{256,192},{320,256},{384,320},{448,384},... | collective-permute-start | bytes 6152 | tf_op jit(solution)/shard_map/ppermute | solution.py:19
  4.7 53.8 %collective-permute-start.31 = (f32[1,8,64]{2,1,0:T(8,128)S(1)}, f32[1,8,64]{2,1,0:T(8,128)S(1)}, u32[]{:S(2)}, u32[]{:S(2)}) collective-permute-start(f32[1,8,64]{2,1,0:T(8,128)S(1)} %broadcast.420), channel_id=1, source_target_pairs={{0,64},{64,128},{128,192},{192,256},{256,320},{320,384},{384,448},... | collective-permute-start | bytes 6152 | tf_op jit(solution)/shard_map/ppermute | solution.py:16
  16.4 15.5 %collective-permute-start.73 = (f32[1,2,16]{2,1,0:T(2,128)S(1)}, f32[1,2,16]{2,1,0:T(2,128)S(1)}, u32[]{:S(2)}, u32[]{:S(2)}) collective-permute-start(f32[1,2,16]{2,1,0:T(2,128)S(1)} %multiply_bitcast_fusion), channel_id=1, source_target_pairs={{0,64},{64,128},{128,192},{192,256},{256,320},{320,384},{384,448},... | collective-permute-start | bytes 392 | tf_op jit(solution)/shard_map/ppermute | solution.py:16
  19.2 15.8 %collective-permute-start.72 = (f32[1,2,16]{2,1,0:T(2,128)S(1)}, f32[1,2,16]{2,1,0:T(2,128)S(1)}, u32[]{:S(2)}, u32[]{:S(2)}) collective-permute-start(f32[1,2,16]{2,1,0:T(2,128)S(1)} %multiply_bitcast_fusion), channel_id=1, source_target_pairs={{64,0},{128,64},{192,128},{256,192},{320,256},{384,320},{448,384},... | collective-permute-start | bytes 392 | tf_op jit(solution)/shard_map/ppermute | solution.py:19
  24.4 20.1 %collective-permute-start.54 = (f32[1,4,32]{2,1,0:T(4,128)S(1)}, f32[1,4,32]{2,1,0:T(4,128)S(1)}, u32[]{:S(2)}, u32[]{:S(2)}) collective-permute-start(f32[1,4,32]{2,1,0:T(4,128)S(1)} %broadcast.429), channel_id=1, source_target_pairs={{64,0},{128,64},{192,128},{256,192},{320,256},{384,320},{448,384},... | collective-permute-start | bytes 1544 | tf_op jit(solution)/shard_map/ppermute | solution.py:19
  37.8 12.7 %collective-permute-start.55 = (f32[1,4,32]{2,1,0:T(4,128)S(1)}, f32[1,4,32]{2,1,0:T(4,128)S(1)}, u32[]{:S(2)}, u32[]{:S(2)}) collective-permute-start(f32[1,4,32]{2,1,0:T(4,128)S(1)} %broadcast.429), channel_id=1, source_target_pairs={{0,64},{64,128},{128,192},{192,256},{256,320},{320,384},{384,448},... | collective-permute-start | bytes 1544 | tf_op jit(solution)/shard_map/ppermute | solution.py:16
  42.5 57.5 %collective-permute-start.7 = (f32[1,16,128]{2,1,0:T(8,128)S(1)}, f32[1,16,128]{2,1,0:T(8,128)S(1)}, u32[]{:S(2)}, u32[]{:S(2)}) collective-permute-start(f32[1,16,128]{2,1,0:T(8,128)S(1)} %get-tuple-element.272), channel_id=1, source_target_pairs={{0,64},{64,128},{128,192},{192,256},{256,320},{320,384},{384,448},... | collective-permute-start | bytes 24584 | tf_op jit(solution)/shard_map/ppermute | solution.py:16
  44.5 59.6 %collective-permute-start.6 = (f32[1,16,128]{2,1,0:T(8,128)S(1)}, f32[1,16,128]{2,1,0:T(8,128)S(1)}, u32[]{:S(2)}, u32[]{:S(2)}) collective-permute-start(f32[1,16,128]{2,1,0:T(8,128)S(1)} %get-tuple-element.271), channel_id=1, source_target_pairs={{64,0},{128,64},{192,128},{256,192},{320,256},{384,320},{448,384},... | collective-permute-start | bytes 24584 | tf_op jit(solution)/shard_map/ppermute | solution.py:19
  50.5 41.5 %collective-permute-start = (f32[1,16,128]{2,1,0:T(8,128)S(1)}, f32[1,16,128]{2,1,0:T(8,128)S(1)}, u32[]{:S(2)}, u32[]{:S(2)}) collective-permute-start(f32[1,16,128]{2,1,0:T(8,128)S(1)} %get-tuple-element.270), channel_id=1, source_target_pairs={{0,64},{64,128},{128,192},{192,256},{256,320},{320,384},{384,448},... | collective-permute-start | bytes 24584 | tf_op jit(solution)/shard_map/ppermute | solution.py:16
  52.5 8.0 %collective-permute-start.25 = (f32[1,8,64]{2,1,0:T(8,128)S(1)}, f32[1,8,64]{2,1,0:T(8,128)S(1)}, u32[]{:S(2)}, u32[]{:S(2)}) collective-permute-start(f32[1,8,64]{2,1,0:T(8,128)S(1)} %get-tuple-element.346), channel_id=1, source_target_pairs={{64,0},{128,64},{192,128},{256,192},{320,256},{384,320},{448,384},... | collective-permute-start | bytes 6152 | tf_op jit(solution)/shard_map/ppermute | solution.py:19
  60.5 34.4 %collective-permute-start.1 = (f32[1,16,128]{2,1,0:T(8,128)S(1)}, f32[1,16,128]{2,1,0:T(8,128)S(1)}, u32[]{:S(2)}, u32[]{:S(2)}) collective-permute-start(f32[1,16,128]{2,1,0:T(8,128)S(1)} %get-tuple-element.269), channel_id=1, source_target_pairs={{64,0},{128,64},{192,128},{256,192},{320,256},{384,320},{448,384},... | collective-permute-start | bytes 24584 | tf_op jit(solution)/shard_map/ppermute | solution.py:19
  88.2 185.7 %collective-permute-start.74 = (f32[3,1,16]{2,1,0:T(1,128)S(1)}, f32[3,1,16]{2,1,0:T(1,128)S(1)}, u32[]{:S(2)}, u32[]{:S(2)}) collective-permute-start(f32[3,1,16]{2,1,0:T(1,128)S(1)} %get-tuple-element.374), channel_id=1, source_target_pairs={{16,0},{32,16},{48,32},{0,48},{17,1},{33,17},{49,33},{1,49},{18,2}... | collective-permute-start | bytes 584 | tf_op jit(solution)/shard_map/ppermute | solution.py:19
  92.0 181.9 %collective-permute-start.75 = (f32[3,1,16]{2,1,0:T(1,128)S(1)}, f32[3,1,16]{2,1,0:T(1,128)S(1)}, u32[]{:S(2)}, u32[]{:S(2)}) collective-permute-start(f32[3,1,16]{2,1,0:T(1,128)S(1)} %get-tuple-element.373), channel_id=1, source_target_pairs={{0,16},{16,32},{32,48},{48,0},{1,17},{17,33},{33,49},{49,1},{2,18}... | collective-permute-start | bytes 584 | tf_op jit(solution)/shard_map/ppermute | solution.py:16
  95.0 110.1 %collective-permute-start.56 = (f32[4,1,32]{2,1,0:T(1,128)S(1)}, f32[4,1,32]{2,1,0:T(1,128)S(1)}, u32[]{:S(2)}, u32[]{:S(2)}) collective-permute-start(f32[4,1,32]{2,1,0:T(1,128)S(1)} %get-tuple-element.358), channel_id=1, source_target_pairs={{16,0},{32,16},{48,32},{0,48},{17,1},{33,17},{49,33},{1,49},{18,2}... | collective-permute-start | bytes 1544 | tf_op jit(solution)/shard_map/ppermute | solution.py:19
  119.9 10.3 %collective-permute-start.11 = (f32[10,18,1]{2,1,0:T(8,128)S(1)}, f32[10,18,1]{2,1,0:T(8,128)S(1)}, u32[]{:S(2)}, u32[]{:S(2)}) collective-permute-start(f32[10,18,1]{2,1,0:T(8,128)S(1)} %get-tuple-element.64), channel_id=1, source_target_pairs={{0,1},{1,2},{2,3},{3,4},{4,5},{5,6},{6,7},{7,8},{8,9},{9,10},{10,1... | collective-permute-start | bytes 2168 | tf_op jit(solution)/shard_map/ppermute | solution.py:16
  187.9 19.1 %collective-permute-start.57 = (f32[4,1,32]{2,1,0:T(1,128)S(1)}, f32[4,1,32]{2,1,0:T(1,128)S(1)}, u32[]{:S(2)}, u32[]{:S(2)}) collective-permute-start(f32[4,1,32]{2,1,0:T(1,128)S(1)} %get-tuple-element.357), channel_id=1, source_target_pairs={{0,16},{16,32},{32,48},{48,0},{1,17},{17,33},{33,49},{49,1},{2,18}... | collective-permute-start | bytes 1544 | tf_op jit(solution)/shard_map/ppermute | solution.py:16
  191.1 37.6 %collective-permute-start.51 = (f32[4,1,32]{2,1,0:T(1,128)S(1)}, f32[4,1,32]{2,1,0:T(1,128)S(1)}, u32[]{:S(2)}, u32[]{:S(2)}) collective-permute-start(f32[4,1,32]{2,1,0:T(1,128)S(1)} %get-tuple-element.356), channel_id=1, source_target_pairs={{16,0},{32,16},{48,32},{0,48},{17,1},{33,17},{49,33},{1,49},{18,2}... | collective-permute-start | bytes 1544 | tf_op jit(solution)/shard_map/ppermute | solution.py:19
  211.0 20.7 %collective-permute-start.50 = (f32[4,1,32]{2,1,0:T(1,128)S(1)}, f32[4,1,32]{2,1,0:T(1,128)S(1)}, u32[]{:S(2)}, u32[]{:S(2)}) collective-permute-start(f32[4,1,32]{2,1,0:T(1,128)S(1)} %get-tuple-element.355), channel_id=1, source_target_pairs={{0,16},{16,32},{32,48},{48,0},{1,17},{17,33},{33,49},{49,1},{2,18}... | collective-permute-start | bytes 1544 | tf_op jit(solution)/shard_map/ppermute | solution.py:16
  228.6 38.2 %collective-permute-start.59 = (f32[4,6,1]{2,1,0:T(8,128)S(1)}, f32[4,6,1]{2,1,0:T(8,128)S(1)}, u32[]{:S(2)}, u32[]{:S(2)}) collective-permute-start(f32[4,6,1]{2,1,0:T(8,128)S(1)} %get-tuple-element.342), channel_id=1, source_target_pairs={{0,1},{1,2},{2,3},{3,4},{4,5},{5,6},{6,7},{7,8},{8,9},{9,10},{10,1... | collective-permute-start | bytes 296 | tf_op jit(solution)/shard_map/ppermute | solution.py:16
  247.2 10.4 %collective-permute-start.45 = (f32[6,1,64]{2,1,0:T(1,128)S(1)}, f32[6,1,64]{2,1,0:T(1,128)S(1)}, u32[]{:S(2)}, u32[]{:S(2)}) collective-permute-start(f32[6,1,64]{2,1,0:T(1,128)S(1)} %get-tuple-element.307), channel_id=1, source_target_pairs={{0,16},{16,32},{32,48},{48,0},{1,17},{17,33},{33,49},{49,1},{2,18}... | collective-permute-start | bytes 4616 | tf_op jit(solution)/shard_map/ppermute | solution.py:16
  277.5 8.1 %collective-permute-start.62 = (f32[4,1,32]{2,1,0:T(1,128)S(1)}, f32[4,1,32]{2,1,0:T(1,128)S(1)}, u32[]{:S(2)}, u32[]{:S(2)}) collective-permute-start(f32[4,1,32]{2,1,0:T(1,128)S(1)} %get-tuple-element.354), channel_id=1, source_target_pairs={{16,0},{32,16},{48,32},{0,48},{17,1},{33,17},{49,33},{1,49},{18,2}... | collective-permute-start | bytes 1544 | tf_op jit(solution)/shard_map/ppermute | solution.py:19
  284.4 15.7 %collective-permute-start.76 = (f32[3,4,1]{2,1,0:T(4,128)S(1)}, f32[3,4,1]{2,1,0:T(4,128)S(1)}, u32[]{:S(2)}, u32[]{:S(2)}) collective-permute-start(f32[3,4,1]{2,1,0:T(4,128)S(1)} %get-tuple-element.360), channel_id=1, source_target_pairs={{1,0},{2,1},{3,2},{4,3},{5,4},{6,5},{7,6},{8,7},{9,8},{10,9},{11,1... | collective-permute-start | bytes 152 | tf_op jit(solution)/shard_map/ppermute | solution.py:19
  285.6 14.5 %collective-permute-start.77 = (f32[3,4,1]{2,1,0:T(4,128)S(1)}, f32[3,4,1]{2,1,0:T(4,128)S(1)}, u32[]{:S(2)}, u32[]{:S(2)}) collective-permute-start(f32[3,4,1]{2,1,0:T(4,128)S(1)} %get-tuple-element.359), channel_id=1, source_target_pairs={{0,1},{1,2},{2,3},{3,4},{4,5},{5,6},{6,7},{7,8},{8,9},{9,10},{10,1... | collective-permute-start | bytes 152 | tf_op jit(solution)/shard_map/ppermute | solution.py:16
  320.1 34.7 %all-to-all-start = ((f32[512,1,256]{2,1,0:T(1,128)}), f32[512,1,256]{2,1,0:T(1,128)S(1)}, u32[]{:S(2)}, u32[]{:S(2)}) async-start(f32[512,1,256]{2,1,0:T(1,128)} %reshape.316), calls=%async_computation | async-start | bytes 1048576 | tf_op jit(solution)/shard_map/all_to_all | solution.py:170
  (154 other events, 4540.5 us)
